TPU v7x, 256 devices: a whole 4x4x8 slice. The times are simulated.
256 devices in a mesh: segment: 8 (over z), expert: 32 (over y, x, core).
Axes of the slice: x: 4, y: 4, z: 8, core: 2. Of those that a mesh axis runs over, the one named last changes fastest.
Arguments:
- inputs: bfloat16 [8, 2, 4096, 2048], P('segment', None, 'expert'), may hold values from -6 to 6
- entering: bfloat16 [8, 4096, 2048], P('segment', 'expert'), may hold values from -6 to 6
- weight_in: bfloat16 [8, 32, 704, 2048], P('segment', 'expert'), may hold values from -0.125 to 0.125
- weight_out: bfloat16 [8, 32, 704, 2048], P('segment', 'expert'), may hold values from -0.21875 to 0.21875
- gate_probs: bfloat16 [8, 2, 4096, 2], P('segment', None, 'expert'), may hold values from 0.049804688 to 1
- expert_ids: int32 [8, 2, 4096, 2], P('segment', None, 'expert'), may hold values from 0 to 31, as said below
Outputs:
- grad_in: bfloat16 [8, 32, 704, 2048], P('segment', 'expert')
- grad_out: bfloat16 [8, 32, 704, 2048], P('segment', 'expert')
- prob_grads: bfloat16 [8, 2, 4096, 2], P('segment', None, 'expert')
Inputs may be any that keep to these rules, and one draw needn't show every extreme that they name: `expert_ids`: each token names 2 different experts. In each aligned block of 128 tokens of one section and tick no expert is named by more than 12 tokens, and in every section and tick one expert, the same for all blocks of that section and tick, is named by exactly 12 tokens of every block.
All inputs are finite; a program needn't handle non-finite values.
Results may differ from a plain program's by a relative error of at most 0.0085.
Values may be sent and summed in bfloat16 or wider, within the bound.
A program may use at most 128 MiB of HBM per device.

v0:
```python
import jax
import jax.numpy as jnp
from jax import lax
from jax.sharding import PartitionSpec as P

TICKS = 2


half_root = 0.7071067811865476
density_scale = 0.3989422804014327


def passed_along(block, axis, distance):
    devices = range(lax.axis_size(axis))
    route = [(i - distance, i) for i in devices if i - distance in devices]
    return lax.ppermute(block, axis, route)


def gelu_parts(preact):
    normal_cdf = 0.5 * (1.0 + jax.scipy.special.erf(preact * half_root))
    normal_pdf = density_scale * jnp.exp(-0.5 * preact * preact)
    return (preact * normal_cdf, normal_cdf + preact * normal_pdf)


def slot_places(chosen, experts, capacity):
    flattened = chosen.reshape(-1)
    matches = (flattened[:, None] == jnp.arange(experts, dtype=jnp.int32)[None, :]).astype(
        jnp.int32
    )
    before = jnp.cumsum(matches, axis=0) - matches
    rank_in = jnp.sum(before * matches, axis=1)
    return (flattened * capacity + rank_in).reshape(chosen.shape)


def build_layout(places, slot_count):
    onehot = places[:, :, None] == jnp.arange(slot_count, dtype=jnp.int32)[None, None, :]
    merged = jnp.sum(onehot, axis=1).astype(jnp.bfloat16)
    return (onehot, merged, merged)


def spread_rows(layout, rows):
    return lax.dot_general(
        layout[1], rows, (((0,), (0,)), ((), ())), preferred_element_type=jnp.float32
    ).astype(jnp.bfloat16)


def spread_probs(layout, probs):
    weighted = jnp.where(layout[0], probs.astype(jnp.float32)[:, :, None], 0.0)
    return jnp.sum(weighted, axis=(0, 1)).astype(jnp.bfloat16)


def collect_rows(layout, returned):
    return jnp.dot(layout[1], returned, preferred_element_type=jnp.float32)


def collect_scores(layout, scores):
    picked = jnp.where(layout[0], scores.astype(jnp.float32)[None, None, :], 0.0)
    return jnp.sum(picked, axis=2).astype(jnp.bfloat16)


def expert_pass(rows_x, rows_g, rows_p, w_in, w_out, need_rows):
    contract_feat = (((1,), (1,)), ((), ()))
    contract_rows = (((0,), (0,)), ((), ()))
    preact = lax.dot_general(rows_x, w_in, contract_feat, preferred_element_type=jnp.float32)
    activated, gate_slope = gelu_parts(preact)
    hidden = activated.astype(jnp.bfloat16)
    pulled = lax.dot_general(rows_g, w_out, contract_feat, preferred_element_type=jnp.float32)
    weight_col = rows_p.astype(jnp.float32)[:, None]
    scores = jnp.sum(hidden.astype(jnp.float32) * pulled, axis=1).astype(jnp.bfloat16)
    grad_pre = (weight_col * pulled * gate_slope).astype(jnp.bfloat16)
    grad_y = (weight_col * rows_g.astype(jnp.float32)).astype(jnp.bfloat16)
    part_out = lax.dot_general(hidden, grad_y, contract_rows, preferred_element_type=jnp.float32)
    part_in = lax.dot_general(grad_pre, rows_x, contract_rows, preferred_element_type=jnp.float32)
    returned = None
    if need_rows:
        returned = jnp.dot(grad_pre, w_in, preferred_element_type=jnp.float32).astype(jnp.bfloat16)
    return (returned, scores, part_in, part_out)


def body(inputs, entering, weight_in, weight_out, gate_probs, expert_ids):
    experts = lax.axis_size("expert")
    rows_local = entering.shape[1]
    features = entering.shape[2]
    top_count = expert_ids.shape[3]
    capacity = 3 * rows_local * top_count // (2 * experts)
    slot_count = experts * capacity
    w_in = weight_in[0, 0]
    w_out = weight_out[0, 0]
    layouts = [
        build_layout(slot_places(expert_ids[0, moment], experts, capacity), slot_count)
        for moment in range(TICKS)
    ]
    total_in = jnp.zeros(w_in.shape, jnp.float32)
    total_out = jnp.zeros(w_out.shape, jnp.float32)
    prob_parts = []
    incoming = entering[0]
    for moment in range(TICKS):
        layout = layouts[moment]
        final_tick = moment + 1 == TICKS
        slots_g = spread_rows(layout, incoming).reshape(experts, capacity, features)
        slots_x = spread_rows(layout, inputs[0, moment]).reshape(experts, capacity, features)
        slots_p = spread_probs(layout, gate_probs[0, moment]).reshape(experts, capacity)
        arrived_x, arrived_g, arrived_p = (
            lax.all_to_all(slots_x, "expert", split_axis=0, concat_axis=0, tiled=True),
            lax.all_to_all(slots_g, "expert", split_axis=0, concat_axis=0, tiled=True),
            lax.all_to_all(slots_p, "expert", split_axis=0, concat_axis=0, tiled=True),
        )
        returned, scores, part_in, part_out = expert_pass(
            arrived_x.reshape(slot_count, features),
            arrived_g.reshape(slot_count, features),
            arrived_p.reshape(slot_count),
            w_in,
            w_out,
            not final_tick,
        )
        total_in = total_in + part_in
        total_out = total_out + part_out
        if final_tick:
            back_scores = lax.all_to_all(
                scores.reshape(experts, capacity), "expert", split_axis=0, concat_axis=0, tiled=True
            )
        else:
            back_rows, back_scores = (
                lax.all_to_all(
                    returned.reshape(experts, capacity, features),
                    "expert",
                    split_axis=0,
                    concat_axis=0,
                    tiled=True,
                ),
                lax.all_to_all(
                    scores.reshape(experts, capacity),
                    "expert",
                    split_axis=0,
                    concat_axis=0,
                    tiled=True,
                ),
            )
            summed = collect_rows(layout, back_rows.reshape(slot_count, features))
            leaving = (incoming.astype(jnp.float32) + summed).astype(jnp.bfloat16)
            incoming = passed_along(leaving, "segment", -1)
        prob_parts.append(collect_scores(layout, back_scores.reshape(slot_count)))
    grad_in = total_in.astype(jnp.bfloat16)[None, None]
    grad_out = total_out.astype(jnp.bfloat16)[None, None]
    prob_grads = jnp.stack(prob_parts)[None]
    return (grad_in, grad_out, prob_grads)


def solution(mesh):
    return jax.shard_map(
        body,
        mesh=mesh,
        in_specs=(
            P("segment", None, "expert", None),
            P("segment", "expert", None),
            P("segment", "expert", None, None),
            P("segment", "expert", None, None),
            P("segment", None, "expert", None),
            P("segment", None, "expert", None),
        ),
        out_specs=(
            P("segment", "expert", None, None),
            P("segment", "expert", None, None),
            P("segment", None, "expert", None),
        ),
        check_vma=False,
    )
```

profile of v0, /device:TPU:1, one launch (start us, length us, event | category | flops | bytes accessed | tf_op | source)
XLA Modules:
  0.0 275.9 jit_solution(8559438610401602208)
XLA Ops:
  9.6 8.6 %all-to-all-start.2 = ((bf16[32,12,2048]{2,1,0:T(8,128)(2,1)}), bf16[32,12,2048]{2,1,0:T(8,128)(2,1)}, u32[]{:S(2)}, u32[]{:S(2)}) async-start(bf16[32,12,2048]{2,1,0:T(8,128)(2,1)} %reshape.223), calls=%async_computation.2 | async-start | bytes 4194304 | tf_op jit(solution)/shard_map/all_to_all | solution.py:104
  24.6 22.3 %all-to-all-done.2 = bf16[32,12,2048]{2,1,0:T(8,128)(2,1)} async-done(((bf16[32,12,2048]{2,1,0:T(8,128)(2,1)}), bf16[32,12,2048]{2,1,0:T(8,128)(2,1)}, u32[]{:S(2)}, u32[]{:S(2)}) %all-to-all-start.2) | async-done | bytes 1572896 | tf_op jit(solution)/shard_map/all_to_all | solution.py:104
  46.9 6.0 %all-to-all-start.1 = ((bf16[32,12,2048]{2,1,0:T(8,128)(2,1)}), bf16[32,12,2048]{2,1,0:T(8,128)(2,1)}, u32[]{:S(2)}, u32[]{:S(2)}) async-start(bf16[32,12,2048]{2,1,0:T(8,128)(2,1)} %reshape.221), calls=%async_computation.1 | async-start | bytes 4194304 | tf_op jit(solution)/shard_map/all_to_all | solution.py:105
  52.9 3.6 %reshape.224 = bf16[384,2048]{1,0:T(8,128)(2,1)} reshape(bf16[32,12,2048]{2,1,0:T(8,128)(2,1)} %all-to-all-done.2) | data formatting | bytes 3145728 | tf_op jit(solution)/shard_map/reshape | solution.py:109
  56.5 4.1 %fusion.6 = f32[384,704]{0,1:T(8,128)} fusion(bf16[384,2048]{1,0:T(8,128)(2,1)} %reshape.224, bf16[1,1,704,2048]{3,2,1,0:T(8,128)(2,1)S(1)} %copy-done), kind=kOutput, calls=%fused_computation.10 | convolution fusion | flops 1107296256 | bytes 5537792 | tf_op jit(solution)/shard_map/dot_general | solution.py:64
  60.6 20.6 %all-to-all-done.1 = bf16[32,12,2048]{2,1,0:T(8,128)(2,1)} async-done(((bf16[32,12,2048]{2,1,0:T(8,128)(2,1)}), bf16[32,12,2048]{2,1,0:T(8,128)(2,1)}, u32[]{:S(2)}, u32[]{:S(2)}) %all-to-all-start.1) | async-done | bytes 1572896 | tf_op jit(solution)/shard_map/all_to_all | solution.py:105
  81.3 3.6 %reshape.222 = bf16[384,2048]{1,0:T(8,128)(2,1)} reshape(bf16[32,12,2048]{2,1,0:T(8,128)(2,1)} %all-to-all-done.1) | data formatting | bytes 3145728 | tf_op jit(solution)/shard_map/reshape | solution.py:110
  84.9 5.4 %multiply_reduce_fusion.1 = (bf16[384]{0:T(512)(128)(2,1)S(1)}, f32[384,704]{0,1:T(8,128)}) fusion(f32[384,704]{0,1:T(8,128)} %fusion.6, bf16[384,2048]{1,0:T(8,128)(2,1)} %reshape.222, bf16[1,1,704,2048]{3,2,1,0:T(8,128)(2,1)} %param.9), kind=kOutput, calls=%fused_computation.41 | convolution fusion | flops 1109458560 | bytes 6619904 | tf_op jit(solution)/shard_map/dot_general | solution.py:67
  91.0 5.6 %all-to-all-start.7 = ((bf16[32,1,12]{2,1,0:T(2,128)(2,1)}), bf16[32,1,12]{2,1,0:T(2,128)(2,1)S(1)}, u32[]{:S(2)}, u32[]{:S(2)}) async-start(bf16[32,1,12]{2,1,0:T(2,128)(2,1)} %convert_element_type.284), calls=%async_computation.7 | async-start | bytes 32768 | tf_op jit(solution)/shard_map/all_to_all | solution.py:131
  96.6 7.0 %all-to-all-done.7 = bf16[32,1,12]{2,1,0:T(2,128)(2,1)S(1)} async-done(((bf16[32,1,12]{2,1,0:T(2,128)(2,1)}), bf16[32,1,12]{2,1,0:T(2,128)(2,1)S(1)}, u32[]{:S(2)}, u32[]{:S(2)}) %all-to-all-start.7) | async-done | bytes 800 | tf_op jit(solution)/shard_map/all_to_all | solution.py:131
  104.1 10.7 %all_to_all.49 = bf16[32,1,12]{2,1,0:T(2,128)(2,1)S(1)} all-to-all(bf16[32,1,12]{2,1,0:T(2,128)(2,1)S(1)} %convert_element_type.282), channel_id=1, replica_groups=mesh['segment'=8,'expert'=32] {'expert'}, dimensions={0} | all-to-all | bytes 1536 | tf_op jit(solution)/shard_map/all_to_all | solution.py:106
  115.0 4.3 %fusion.12 = bf16[384,2048]{1,0:T(8,128)(2,1)} fusion(bf16[1,1,704,2048]{3,2,1,0:T(8,128)(2,1)S(1)} %copy-done, f32[384,704]{0,1:T(8,128)} %fusion.6, f32[384,704]{0,1:T(8,128)} %get-tuple-element.12, f32[384]{0:T(512)S(1)} %reshape.233), kind=kOutput, calls=%fused_computation.16 | convolution fusion | flops 1111056384 | bytes 6620672 | tf_op jit(solution)/shard_map/dot_general | solution.py:76
  119.3 3.6 %reshape.226 = bf16[32,12,2048]{2,1,0:T(8,128)(2,1)} reshape(bf16[384,2048]{1,0:T(8,128)(2,1)} %fusion.12) | data formatting | bytes 3145728 | tf_op jit(solution)/shard_map/reshape | solution.py:125
  122.9 5.0 %all-to-all-start.4 = ((bf16[32,12,2048]{2,1,0:T(8,128)(2,1)}), bf16[32,12,2048]{2,1,0:T(8,128)(2,1)}, u32[]{:S(2)}, u32[]{:S(2)}) async-start(bf16[32,12,2048]{2,1,0:T(8,128)(2,1)} %reshape.226), calls=%async_computation.4 | async-start | bytes 4194304 | tf_op jit(solution)/shard_map/all_to_all | solution.py:124
  136.0 20.3 %all-to-all-done.4 = bf16[32,12,2048]{2,1,0:T(8,128)(2,1)} async-done(((bf16[32,12,2048]{2,1,0:T(8,128)(2,1)}), bf16[32,12,2048]{2,1,0:T(8,128)(2,1)}, u32[]{:S(2)}, u32[]{:S(2)}) %all-to-all-start.4) | async-done | bytes 1572896 | tf_op jit(solution)/shard_map/all_to_all | solution.py:124
  156.3 6.5 %all-to-all-start.6 = ((bf16[32,12,2048]{2,1,0:T(8,128)(2,1)}), bf16[32,12,2048]{2,1,0:T(8,128)(2,1)}, u32[]{:S(2)}, u32[]{:S(2)}) async-start(bf16[32,12,2048]{2,1,0:T(8,128)(2,1)} %reshape.230), calls=%async_computation.6 | async-start | bytes 4194304 | tf_op jit(solution)/shard_map/all_to_all | solution.py:104
  162.7 3.6 %reshape.227 = bf16[384,2048]{1,0:T(8,128)(2,1)} reshape(bf16[32,12,2048]{2,1,0:T(8,128)(2,1)} %all-to-all-done.4) | data formatting | bytes 3145728 | tf_op jit(solution)/shard_map/reshape | solution.py:139
  169.8 14.0 %collective-permute-done = bf16[128,2048]{1,0:T(8,128)(2,1)S(1)} collective-permute-done((bf16[128,2048]{1,0:T(8,128)(2,1)S(1)}, bf16[128,2048]{1,0:T(8,128)(2,1)S(1)}, u32[]{:S(2)}, u32[]{:S(2)}) %collective-permute-start) | collective-permute-done | bytes 524320 | tf_op jit(solution)/shard_map/ppermute | solution.py:16
  185.5 3.6 %reshape.228 = bf16[32,12,2048]{2,1,0:T(8,128)(2,1)} reshape(bf16[384,2048]{1,0:T(8,128)(2,1)} %convolution_convert_fusion.1) | data formatting | bytes 3145728 | tf_op jit(solution)/shard_map/reshape | solution.py:100
  191.1 6.5 %all-to-all-start.5 = ((bf16[32,12,2048]{2,1,0:T(8,128)(2,1)}), bf16[32,12,2048]{2,1,0:T(8,128)(2,1)}, u32[]{:S(2)}, u32[]{:S(2)}) async-start(bf16[32,12,2048]{2,1,0:T(8,128)(2,1)} %reshape.228), calls=%async_computation.5 | async-start | bytes 4194304 | tf_op jit(solution)/shard_map/all_to_all | solution.py:105
  197.6 3.7 %reshape.231 = bf16[384,2048]{1,0:T(8,128)(2,1)} reshape(bf16[32,12,2048]{2,1,0:T(8,128)(2,1)} %all-to-all-done.6) | data formatting | bytes 3145728 | tf_op jit(solution)/shard_map/reshape | solution.py:109
  201.2 4.2 %fusion.2 = f32[384,704]{0,1:T(8,128)} fusion(bf16[384,2048]{1,0:T(8,128)(2,1)} %reshape.231, bf16[1,1,704,2048]{3,2,1,0:T(8,128)(2,1)S(1)} %copy-done), kind=kOutput, calls=%fused_computation.6 | convolution fusion | flops 1107296256 | bytes 5537792 | tf_op jit(solution)/shard_map/dot_general | solution.py:64
  205.5 4.3 %fusion.56 = f32[704,2048]{1,0:T(8,128)} fusion(bf16[384,2048]{1,0:T(8,128)(2,1)S(1)} %copy-done.1, f32[384,704]{0,1:T(8,128)S(1)} %copy-done.3, f32[384,704]{0,1:T(8,128)S(1)} %copy-done.5, f32[384]{0:T(512)S(1)} %reshape.233), kind=kOutput, calls=%fused_computation.98 | convolution fusion | flops 1110269952 | bytes 9504256 | tf_op jit(solution)/shard_map/dot_general | solution.py:73
  209.8 16.2 %all-to-all-done.5 = bf16[32,12,2048]{2,1,0:T(8,128)(2,1)} async-done(((bf16[32,12,2048]{2,1,0:T(8,128)(2,1)}), bf16[32,12,2048]{2,1,0:T(8,128)(2,1)}, u32[]{:S(2)}, u32[]{:S(2)}) %all-to-all-start.5) | async-done | bytes 1572896 | tf_op jit(solution)/shard_map/all_to_all | solution.py:105
  226.0 3.6 %reshape.229 = bf16[384,2048]{1,0:T(8,128)(2,1)} reshape(bf16[32,12,2048]{2,1,0:T(8,128)(2,1)} %all-to-all-done.5) | data formatting | bytes 3145728 | tf_op jit(solution)/shard_map/reshape | solution.py:110
  229.6 5.2 %multiply_reduce_fusion = (bf16[384]{0:T(512)(128)(2,1)S(1)}, f32[384,704]{0,1:T(8,128)}) fusion(f32[384,704]{0,1:T(8,128)} %fusion.2, bf16[384,2048]{1,0:T(8,128)(2,1)} %reshape.229, bf16[1,1,704,2048]{3,2,1,0:T(8,128)(2,1)} %param.9), kind=kOutput, calls=%fused_computation.40 | convolution fusion | flops 1109458560 | bytes 6619904 | tf_op jit(solution)/shard_map/dot_general | solution.py:67
  235.5 5.6 %all-to-all-start.8 = ((bf16[32,1,12]{2,1,0:T(2,128)(2,1)}), bf16[32,1,12]{2,1,0:T(2,128)(2,1)S(1)}, u32[]{:S(2)}, u32[]{:S(2)}) async-start(bf16[32,1,12]{2,1,0:T(2,128)(2,1)} %convert_element_type.285), calls=%async_computation.8 | async-start | bytes 32768 | tf_op jit(solution)/shard_map/all_to_all | solution.py:119
  241.1 6.1 %fusion.16 = f32[704,2048]{1,0:T(8,128)} fusion(bf16[384,2048]{1,0:T(8,128)(2,1)} %reshape.222, f32[384]{0:T(512)S(1)} %reshape.233, f32[384,704]{0,1:T(8,128)} %fusion.6), kind=kOutput, calls=%fused_computation.25 | convolution fusion | flops 1111007232 | bytes 8422912 | tf_op jit(solution)/shard_map/dot_general | solution.py:72
  249.3 6.5 %all-to-all-start.3 = ((bf16[32,1,12]{2,1,0:T(2,128)(2,1)}), bf16[32,1,12]{2,1,0:T(2,128)(2,1)S(1)}, u32[]{:S(2)}, u32[]{:S(2)}) async-start(bf16[32,1,12]{2,1,0:T(2,128)(2,1)} %convert_element_type.283), calls=%async_computation.3 | async-start | bytes 32768 | tf_op jit(solution)/shard_map/all_to_all | solution.py:106
  256.4 6.3 %all-to-all-done.3 = bf16[32,1,12]{2,1,0:T(2,128)(2,1)S(1)} async-done(((bf16[32,1,12]{2,1,0:T(2,128)(2,1)}), bf16[32,1,12]{2,1,0:T(2,128)(2,1)S(1)}, u32[]{:S(2)}, u32[]{:S(2)}) %all-to-all-start.3) | async-done | bytes 800 | tf_op jit(solution)/shard_map/all_to_all | solution.py:106
  262.9 6.9 %fusion.1 = bf16[1,1,704,2048]{3,2,1,0:T(8,128)(2,1)} fusion(f32[704,2048]{1,0:T(8,128)} %fusion.16, bf16[384,2048]{1,0:T(8,128)(2,1)} %reshape.229, f32[384]{0:T(512)S(1)} %reshape.235, f32[384,704]{0,1:T(8,128)} %fusion.2), kind=kOutput, calls=%fused_computation.5 | convolution fusion | flops 1113890816 | bytes 11306496 | tf_op jit(solution)/shard_map/dot_general | solution.py:72
  269.8 6.1 %fusion = bf16[1,1,704,2048]{3,2,1,0:T(8,128)(2,1)} fusion(f32[704,2048]{1,0:T(8,128)} %fusion.56, bf16[384,2048]{1,0:T(8,128)(2,1)S(1)} %copy-done.2, f32[384,704]{0,1:T(8,128)S(1)} %copy-done.4, f32[384,704]{0,1:T(8,128)S(1)} %copy-done.6, f32[384]{0:T(512)S(1)} %reshape.235), kind=kOutput, calls=%fused_computation.4 | convolution fusion | flops 1113153536 | bytes 12387840 | tf_op jit(solution)/shard_map/dot_general | solution.py:73
  (70 shorter events, 35.4 us)
Async XLA Ops:
  0.6 55.9 %copy-start = (bf16[1,1,704,2048]{3,2,1,0:T(8,128)(2,1)S(1)}, bf16[1,1,704,2048]{3,2,1,0:T(8,128)(2,1)}, u32[]{:S(2)}) copy-start(bf16[1,1,704,2048]{3,2,1,0:T(8,128)(2,1)} %param.8) | copy-start | bytes 8650756
  9.6 37.4 %all-to-all-start.2 = ((bf16[32,12,2048]{2,1,0:T(8,128)(2,1)}), bf16[32,12,2048]{2,1,0:T(8,128)(2,1)}, u32[]{:S(2)}, u32[]{:S(2)}) async-start(bf16[32,12,2048]{2,1,0:T(8,128)(2,1)} %reshape.223), calls=%async_computation.2 | async-start | bytes 4194304 | tf_op jit(solution)/shard_map/all_to_all | solution.py:104
  46.9 34.3 %all-to-all-start.1 = ((bf16[32,12,2048]{2,1,0:T(8,128)(2,1)}), bf16[32,12,2048]{2,1,0:T(8,128)(2,1)}, u32[]{:S(2)}, u32[]{:S(2)}) async-start(bf16[32,12,2048]{2,1,0:T(8,128)(2,1)} %reshape.221), calls=%async_computation.1 | async-start | bytes 4194304 | tf_op jit(solution)/shard_map/all_to_all | solution.py:105
  84.9 11.7 %copy-start.7 = (bf16[1,2,128,2]{2,3,1,0:T(2,128)(2,1)S(1)}, bf16[1,2,128,2]{2,3,1,0:T(2,128)(2,1)}, u32[]{:S(2)}) copy-start(bf16[1,2,128,2]{2,3,1,0:T(2,128)(2,1)} %param.10) | copy-start | bytes 3076
  91.0 12.6 %all-to-all-start.7 = ((bf16[32,1,12]{2,1,0:T(2,128)(2,1)}), bf16[32,1,12]{2,1,0:T(2,128)(2,1)S(1)}, u32[]{:S(2)}, u32[]{:S(2)}) async-start(bf16[32,1,12]{2,1,0:T(2,128)(2,1)} %convert_element_type.284), calls=%async_computation.7 | async-start | bytes 32768 | tf_op jit(solution)/shard_map/all_to_all | solution.py:131
  122.9 33.4 %all-to-all-start.4 = ((bf16[32,12,2048]{2,1,0:T(8,128)(2,1)}), bf16[32,12,2048]{2,1,0:T(8,128)(2,1)}, u32[]{:S(2)}, u32[]{:S(2)}) async-start(bf16[32,12,2048]{2,1,0:T(8,128)(2,1)} %reshape.226), calls=%async_computation.4 | async-start | bytes 4194304 | tf_op jit(solution)/shard_map/all_to_all | solution.py:124
  156.3 34.8 %all-to-all-start.6 = ((bf16[32,12,2048]{2,1,0:T(8,128)(2,1)}), bf16[32,12,2048]{2,1,0:T(8,128)(2,1)}, u32[]{:S(2)}, u32[]{:S(2)}) async-start(bf16[32,12,2048]{2,1,0:T(8,128)(2,1)} %reshape.230), calls=%async_computation.6 | async-start | bytes 4194304 | tf_op jit(solution)/shard_map/all_to_all | solution.py:104
  168.3 15.4 %collective-permute-start = (bf16[128,2048]{1,0:T(8,128)(2,1)S(1)}, bf16[128,2048]{1,0:T(8,128)(2,1)S(1)}, u32[]{:S(2)}, u32[]{:S(2)}) collective-permute-start(bf16[128,2048]{1,0:T(8,128)(2,1)S(1)} %fusion.15), channel_id=1, source_target_pairs={{32,0},{64,32},{96,64},{128,96},{160,128},{192,160},{224,192},{33,... | collective-permute-start | bytes 1572872 | tf_op jit(solution)/shard_map/ppermute | solution.py:16
  191.1 34.8 %all-to-all-start.5 = ((bf16[32,12,2048]{2,1,0:T(8,128)(2,1)}), bf16[32,12,2048]{2,1,0:T(8,128)(2,1)}, u32[]{:S(2)}, u32[]{:S(2)}) async-start(bf16[32,12,2048]{2,1,0:T(8,128)(2,1)} %reshape.228), calls=%async_computation.5 | async-start | bytes 4194304 | tf_op jit(solution)/shard_map/all_to_all | solution.py:105
  201.2 4.2 %copy-start.1 = (bf16[384,2048]{1,0:T(8,128)(2,1)S(1)}, bf16[384,2048]{1,0:T(8,128)(2,1)}, u32[]{:S(2)}) copy-start(bf16[384,2048]{1,0:T(8,128)(2,1)} %reshape.224) | copy-start | bytes 4718596
  201.2 4.2 %copy-start.3 = (f32[384,704]{0,1:T(8,128)S(1)}, f32[384,704]{0,1:T(8,128)}, u32[]{:S(2)}) copy-start(f32[384,704]{0,1:T(8,128)} %fusion.6) | copy-start | bytes 3244036
  201.2 4.2 %copy-start.5 = (f32[384,704]{0,1:T(8,128)S(1)}, f32[384,704]{0,1:T(8,128)}, u32[]{:S(2)}) copy-start(f32[384,704]{0,1:T(8,128)} %get-tuple-element.12) | copy-start | bytes 3244036
  235.5 12.6 %all-to-all-start.8 = ((bf16[32,1,12]{2,1,0:T(2,128)(2,1)}), bf16[32,1,12]{2,1,0:T(2,128)(2,1)S(1)}, u32[]{:S(2)}, u32[]{:S(2)}) async-start(bf16[32,1,12]{2,1,0:T(2,128)(2,1)} %convert_element_type.285), calls=%async_computation.8 | async-start | bytes 32768 | tf_op jit(solution)/shard_map/all_to_all | solution.py:119
  249.3 13.4 %all-to-all-start.3 = ((bf16[32,1,12]{2,1,0:T(2,128)(2,1)}), bf16[32,1,12]{2,1,0:T(2,128)(2,1)S(1)}, u32[]{:S(2)}, u32[]{:S(2)}) async-start(bf16[32,1,12]{2,1,0:T(2,128)(2,1)} %convert_element_type.283), calls=%async_computation.3 | async-start | bytes 32768 | tf_op jit(solution)/shard_map/all_to_all | solution.py:106
  262.9 7.0 %copy-start.2 = (bf16[384,2048]{1,0:T(8,128)(2,1)S(1)}, bf16[384,2048]{1,0:T(8,128)(2,1)}, u32[]{:S(2)}) copy-start(bf16[384,2048]{1,0:T(8,128)(2,1)} %reshape.231) | copy-start | bytes 4718596
  262.9 7.0 %copy-start.4 = (f32[384,704]{0,1:T(8,128)S(1)}, f32[384,704]{0,1:T(8,128)}, u32[]{:S(2)}) copy-start(f32[384,704]{0,1:T(8,128)} %fusion.2) | copy-start | bytes 3244036
  262.9 6.9 %copy-start.6 = (f32[384,704]{0,1:T(8,128)S(1)}, f32[384,704]{0,1:T(8,128)}, u32[]{:S(2)}) copy-start(f32[384,704]{0,1:T(8,128)} %get-tuple-element.14) | copy-start | bytes 3244036
where the time goes:
time: 278 us; the launch traced here: 276 us
  waiting for transfers between devices  110 us (40%)
  matrix products  58.6 us (21%)
  starting transfers between devices  51.8 us (19%)
  local copies, waits for them, and re-layouts  41.3 us (15%)
  blocking collectives  10.7 us (4%)
  other arithmetic  2.96 us (1%)
    all_to_all x2, waiting for transfers between devices, body(): lax.all_to_all(slots_g, 'expert', split_axis=0, concat_axis=0, tiled=True)  36.8 us
    all_to_all x2, waiting for transfers between devices, body(): lax.all_to_all(slots_x, 'expert', split_axis=0, concat_axis=0, tiled=True)  24.4 us
    all_to_all x1, waiting for transfers between devices, body(): lax.all_to_all(returned.reshape(experts, capacity, features), 'expert', s...  20.3 us
    all_to_all x2, starting transfers between devices, body(): lax.all_to_all(slots_x, 'expert', split_axis=0, concat_axis=0, tiled=True)  15.1 us
    ppermute x1, waiting for transfers between devices, passed_along(): return lax.ppermute(block, axis, route)  14 us
    dot_general x2, matrix products, expert_pass(): lax.dot_general(hidden, grad_y, contract_rows, preferred_element_type=jnp...  13 us
    all_to_all x2, starting transfers between devices, body(): lax.all_to_all(slots_g, 'expert', split_axis=0, concat_axis=0, tiled=True)  12.4 us
    all_to_all x2, starting transfers between devices, body(): lax.all_to_all(scores.reshape(experts, capacity), 'expert', split_axis=0,...  11.2 us
  transfers between devices with their start and end apart: 9, of which 9 were waited for; matrix products, arithmetic and copies ran while one was open for 19% of the time, Pallas kernels for 0%

commit v1 on v0

v1 whole, which is shorter than its diff:
```python
import jax
import jax.numpy as jnp
from jax import lax
from jax.experimental import pallas as pl
from jax.experimental.pallas import tpu as pltpu
from jax.sharding import PartitionSpec as P

MESH = pl.DeviceIdType.MESH
F32 = jnp.float32
BF16 = jnp.bfloat16
NT = (((1,), (1,)), ((), ()))
FF = 704
D = 2048
TOK = 128
PEERS = 32
ROWS = 256
WIDE = 3072
HALF = 192
HR = 0.7071067811865476
DS = 0.3989422804014327


def iota(shape, dim):
    return lax.broadcasted_iota(jnp.int32, shape, dim)


def dot(a, b):
    return jnp.dot(a, b, preferred_element_type=F32)


def dot_nt(a, b):
    return lax.dot_general(a, b, NT, preferred_element_type=F32)


def onehot(cond):
    return jnp.where(cond, 1.0, 0.0)


def kernel(
    inputs_hbm, entering_hbm, win_hbm, wout_hbm, probs_ref, ids_ref,
    gin_hbm, gout_hbm, pg_ref,
    xin, g0, win, wout,
    sx0, sg, sx1, rs,
    xr0, gr0, xr1, rr, gr1,
    xc, gc, ht, gp, slope, gpr, rb,
    acco, acci, outo, outi,
    lv_send, lv_recv, s_send, s_recv,
    da, dap, ca, cols,
    send_sem, recv_sem, z_send, z_recv, local_sem, out_sem,
):
    me = lax.axis_index("expert")
    seg = lax.axis_index("segment")
    core = lax.rem(me, 2)
    px = lax.rem(lax.div(me, 2), 4)
    py = lax.div(me, 8)

    def steps(k):
        dc = lax.rem(k, 2)
        dx = lax.rem(lax.div(k, 2), 4)
        dy = lax.rem(lax.div(k, 8) + dx, 4)
        return dy, dx, dc

    def ahead(k):
        dy, dx, dc = steps(k)
        return lax.rem(py + dy, 4) * 8 + lax.rem(px + dx, 4) * 2 + lax.rem(core + dc, 2)

    def behind(k):
        dy, dx, dc = steps(k)
        return lax.rem(py + 4 - dy, 4) * 8 + lax.rem(px + 4 - dx, 4) * 2 + lax.rem(core + dc, 2)

    def copy(stage, src, dst, k, peer):
        rows = pl.ds(pl.multiple_of(k * 8, 8), 8)
        return pltpu.make_async_remote_copy(
            src_ref=src.at[rows], dst_ref=dst.at[rows],
            send_sem=send_sem.at[stage, k], recv_sem=recv_sem.at[stage, k],
            device_id=(seg, peer), device_id_type=MESH,
        )

    def send(stage, src, dst, route, low, high):
        def one(k, carry):
            copy(stage, src, dst, k, route(k)).start()
            return carry
        lax.fori_loop(max(low, 1), high, one, 0)

    def arrive(stage, src, dst, low, high):
        def one(k, carry):
            copy(stage, src, dst, k, ahead(k)).wait_recv()
            return carry
        lax.fori_loop(max(low, 1), high, one, 0)

    def sent(stage, src, dst):
        def one(k, carry):
            copy(stage, src, dst, k, ahead(k)).wait_send()
            return carry
        lax.fori_loop(1, PEERS, one, 0)

    load_g = pltpu.make_async_copy(entering_hbm, g0, local_sem.at[0])
    load_x = pltpu.make_async_copy(inputs_hbm, xin, local_sem.at[1])
    load_wi = pltpu.make_async_copy(win_hbm, win, local_sem.at[2])
    load_wo = pltpu.make_async_copy(wout_hbm, wout, local_sem.at[3])
    load_x.start()
    load_g.start()
    load_wi.start()
    load_wo.start()

    barrier = pltpu.get_barrier_semaphore()

    def greet(k, carry):
        pl.semaphore_signal(barrier, inc=1, device_id=(seg, ahead(k)), device_id_type=MESH)
        return carry

    lax.fori_loop(1, PEERS, greet, 0)
    below = lax.rem(seg + 7, 8)
    above = lax.rem(seg + 1, 8)
    pl.semaphore_signal(barrier, inc=1, device_id=(below, me), device_id_type=MESH)
    pl.semaphore_signal(barrier, inc=1, device_id=(above, me), device_id_type=MESH)

    def places(tick):
        ids = ids_ref[tick]
        k = iota((TOK, 128), 1)
        dx = (k >> 1) & 3
        dy = ((k >> 3) + dx) & 3
        owner = ((py + dy) & 3) * 8 + ((px + dx) & 3) * 2 + ((core + (k & 1)) & 1)
        owner = jnp.where(k < PEERS, owner, -1)
        named = [ids[:, j : j + 1] == owner for j in range(2)]
        either = onehot(named[0] | named[1]).astype(BF16)
        earlier = onehot(iota((TOK, TOK), 1) < iota((TOK, TOK), 0)).astype(BF16)
        count = dot(earlier, either)
        first = (k * 8).astype(F32)
        probs = probs_ref[tick].astype(F32)
        packed = jnp.zeros((TOK, 128), F32)
        for j in range(2):
            rank = jnp.sum(jnp.where(named[j], count, 0.0), axis=1, keepdims=True)
            base = jnp.sum(jnp.where(named[j], first, 0.0), axis=1, keepdims=True)
            low = jnp.where(rank < 8.0, base + rank, -100.0)
            high = jnp.where(rank < 8.0, -100.0, base + rank - 8.0)
            packed = jnp.where(k == j, low, packed)
            packed = jnp.where(k == 2 + j, high, packed)
            packed = jnp.where(k == 4 + j, probs[:, j : j + 1], packed)
        cols[tick] = packed
        eye = onehot(iota((8, 128), 0) == iota((8, 128), 1)).astype(BF16)
        turned = dot_nt(eye, packed.astype(BF16))
        slot = iota((ROWS, TOK), 0).astype(F32)
        for part, (row, shift) in enumerate(((0, 0.0), (2, 0.0), (2, 4.0))):
            hit0 = slot == turned[row : row + 1] + shift
            hit1 = slot == turned[row + 1 : row + 2] + shift
            da[part] = onehot(hit0 | hit1).astype(BF16)
            dap[part] = jnp.where(
                hit0, turned[4:5], jnp.where(hit1, turned[5:6], 0.0)
            ).astype(BF16)

    def pick(tick, j, part):
        row, shift = ((0, 0.0), (2, 0.0), (2, 4.0))[part]
        slot = iota((TOK, ROWS), 1).astype(F32)
        return slot == cols[tick, :, row + j : row + j + 1] + shift

    def dispatch(mats, rows, dst):
        for n in range(4):
            c = slice(n * 512, n * 512 + 512)
            dst[:, c] = dot(mats[0], rows[:, c]).astype(BF16)
        for n in range(2):
            c = slice(n * 512, n * 512 + 512)
            h = slice(1024 + n * 512, 1536 + n * 512)
            dst[:, 2048 + n * 512 : 2560 + n * 512] = (
                dot(mats[1], rows[:, c]) + dot(mats[2], rows[:, h])
            ).astype(BF16)

    def split_matrix():
        o = iota((128, 128), 0)
        i = iota((128, 128), 1)
        return onehot(i == ((o & 63) >> 2) * 8 + (o >> 6) * 4 + (o & 3)).astype(BF16)

    def join_matrix():
        i = iota((128, 128), 0)
        o = iota((128, 128), 1)
        return onehot(i == ((o & 63) >> 2) * 8 + (o >> 6) * 4 + (o & 3)).astype(BF16)

    def gather(src, dst, tick, h):
        r = slice(h * 128, h * 128 + 128)
        dst[tick, h, 0:128, :] = src[r, 0:D]
        for n in range(2):
            b = dot(split_matrix(), src[r, D + n * 512 : D + n * 512 + 512]).astype(BF16)
            dst[tick, h, 128:192, n * 512 : n * 512 + 512] = b[0:64]
            dst[tick, h, 128:192, 1024 + n * 512 : 1536 + n * 512] = b[64:128]

    def forward(tick, h):
        def tile(m, carry):
            r = pl.ds(pl.multiple_of(m * 352, 16), 352)
            pre = dot_nt(win[r, :], xc[tick, h])
            cdf = 0.5 * (1.0 + lax.erf(pre * HR))
            pdf = DS * jnp.exp(-0.5 * pre * pre)
            ht[tick, h, r, :] = (pre * cdf).astype(BF16)
            slope[h, r, :] = cdf + pre * pdf
            return carry
        lax.fori_loop(0, 2, tile, 0)

    def backward(tick, h):
        def tile(m, total):
            r = pl.ds(pl.multiple_of(m * 352, 16), 352)
            q = dot_nt(wout[r, :], gc[tick, h])
            gp[tick, h, r, :] = (q * slope[h, r, :]).astype(BF16)
            return total + jnp.sum(ht[tick, h, r, :].astype(F32) * q, axis=0, keepdims=True)
        s = lax.fori_loop(0, 2, tile, jnp.zeros((1, HALF), F32))
        i = iota((128, HALF), 0)
        r = iota((128, HALF), 1)
        ones = jnp.ones((HALF, 128), BF16)
        sa = dot(jnp.where(r == i, s, 0.0).astype(BF16), ones)
        tail = ((i & 7) < 4) & (r == 128 + (i >> 3) * 4 + (i & 7))
        sb = dot(jnp.where(tail, s, 0.0).astype(BF16), ones)
        lane = iota((128, 128), 1)
        rows = slice(h * 128, h * 128 + 128)
        before = jnp.zeros((128, 128), F32) if tick == 0 else s_send[rows, :].astype(F32)
        s_send[rows, :] = jnp.where(
            lane == tick, sa, jnp.where(lane == 2 + tick, sb, before)
        ).astype(BF16)

    def give_back(h):
        eye = onehot(iota((HALF, HALF), 0) == iota((HALF, HALF), 1)).astype(BF16)
        gpr[...] = dot_nt(eye, gp[0, h]).astype(BF16)
        rows = slice(h * 128, h * 128 + 128)

        def tile(n, carry):
            c = pl.ds(pl.multiple_of(n * 512, 512), 512)
            r = dot(gpr[...], win[:, c]).astype(BF16)
            rs[rows, c] = r[0:128]
            rb[:, c] = r[128:192]
            return carry

        lax.fori_loop(0, 4, tile, 0)
        join = join_matrix()
        for n in range(2):
            c = slice(n * 512, n * 512 + 512)
            d = slice(1024 + n * 512, 1536 + n * 512)
            b = dot(join[:, 0:64], rb[:, c]) + dot(join[:, 64:128], rb[:, d])
            rs[rows, D + n * 512 : D + n * 512 + 512] = b.astype(BF16)

    def own(src, dst):
        dst[0:8, :] = src[0:8, :]

    places(0)
    load_x.wait()
    dispatch([da[0], da[1], da[2]], xin.at[0], sx0)
    pl.semaphore_wait(barrier, PEERS + 1)
    send(0, sx0, xr0, ahead, 0, PEERS)
    load_g.wait()
    dispatch([dap[0], dap[1], dap[2]], g0, sg)
    send(1, sg, gr0, ahead, 0, PEERS)
    own(sx0, xr0)
    own(sg, gr0)
    for part in range(3):
        ca[part] = onehot(pick(0, 0, part) | pick(0, 1, part)).astype(BF16)
    places(1)
    dispatch([da[0], da[1], da[2]], xin.at[1], sx1)
    own(sx1, xr1)
    load_wi.wait()
    load_wo.wait()

    for h in range(2):
        arrive(0, sx0, xr0, h * 16, h * 16 + 16)
        gather(xr0, xc, 0, h)
        forward(0, h)
    for h in range(2):
        arrive(1, sg, gr0, h * 16, h * 16 + 16)
        gather(gr0, gc, 0, h)
        backward(0, h)
        give_back(h)
        send(2, rs, rr, behind, h * 16, h * 16 + 16)
    own(rs, rr)
    send(3, sx1, xr1, ahead, 0, PEERS)

    def first_sums(n, carry):
        c = pl.ds(pl.multiple_of(n * 256, 256), 256)
        acco[:, c] = dot(ht[0, 0], gc[0, 0, :, c]) + dot(ht[0, 1], gc[0, 1, :, c])
        acci[:, c] = dot(gp[0, 0], xc[0, 0, :, c]) + dot(gp[0, 1], xc[0, 1, :, c])
        return carry

    lax.fori_loop(0, 8, first_sums, 0)

    arrive(2, rs, rr, 0, PEERS)
    for n in range(4):
        c = slice(n * 512, n * 512 + 512)
        d = slice(D + (n % 2) * 512, D + (n % 2) * 512 + 512)
        total = g0[:, c].astype(F32) + dot(ca[0], rr[:, c]) + dot(ca[1 + n // 2], rr[:, d])
        lv_send[:, c] = total.astype(BF16)
    relay = pltpu.make_async_remote_copy(
        src_ref=lv_send, dst_ref=lv_recv, send_sem=z_send, recv_sem=z_recv,
        device_id=(below, me), device_id_type=MESH,
    )
    relay.start()
    sent(1, sg, gr0)
    relay.wait_recv()
    for n in range(4):
        c = slice(n * 512, n * 512 + 512)
        v = lv_recv[:, c]
        g0[:, c] = jnp.where(seg == 7, jnp.zeros_like(v), v)
    dispatch([dap[0], dap[1], dap[2]], g0, sg)
    send(4, sg, gr1, ahead, 0, PEERS)
    own(sg, gr1)

    for h in range(2):
        arrive(3, sx1, xr1, h * 16, h * 16 + 16)
        gather(xr1, xc, 1, h)
        forward(1, h)

    arrive(4, sg, gr1, 0, 16)
    gather(gr1, gc, 1, 0)
    backward(1, 0)

    def more_sums(n, carry):
        c = pl.ds(pl.multiple_of(n * 256, 256), 256)
        acco[:, c] += dot(ht[1, 0], gc[1, 0, :, c])
        acci[:, c] += dot(gp[1, 0], xc[1, 0, :, c])
        return carry

    lax.fori_loop(0, 8, more_sums, 0)

    arrive(4, sg, gr1, 16, PEERS)
    gather(gr1, gc, 1, 1)
    backward(1, 1)
    send(5, s_send, s_recv, behind, 0, PEERS)
    own(s_send, s_recv)

    def last_sums(n, carry):
        c = pl.ds(pl.multiple_of(n * 256, 256), 256)
        outo[:, c] = (acco[:, c] + dot(ht[1, 1], gc[1, 1, :, c])).astype(BF16)
        outi[:, c] = (acci[:, c] + dot(gp[1, 1], xc[1, 1, :, c])).astype(BF16)
        pltpu.make_async_copy(outo.at[:, c], gout_hbm.at[:, c], out_sem.at[0, n]).start()
        pltpu.make_async_copy(outi.at[:, c], gin_hbm.at[:, c], out_sem.at[1, n]).start()
        return carry

    lax.fori_loop(0, 8, last_sums, 0)

    arrive(5, s_send, s_recv, 0, PEERS)
    lane = iota((TOK, 128), 1)
    score = s_recv[...]
    for tick in range(2):
        found = []
        for j in range(2):
            va = dot(onehot(pick(tick, j, 0)).astype(BF16), score)
            vb = dot(onehot(pick(tick, j, 1)).astype(BF16), score)
            both = jnp.where(lane == tick, va, 0.0) + jnp.where(lane == 2 + tick, vb, 0.0)
            value = jnp.sum(both, axis=1, keepdims=True)
            found.append(value / cols[tick, :, 4 + j : 5 + j])
        pair = jnp.where(iota((TOK, 2), 1) == 0, found[0], found[1])
        pg_ref[tick] = pair.astype(BF16)

    def out_done(n, carry):
        c = pl.ds(pl.multiple_of(n * 256, 256), 256)
        pltpu.make_async_copy(outo.at[:, c], gout_hbm.at[:, c], out_sem.at[0, n]).wait()
        pltpu.make_async_copy(outi.at[:, c], gin_hbm.at[:, c], out_sem.at[1, n]).wait()
        return carry

    lax.fori_loop(0, 8, out_done, 0)
    relay.wait_send()
    sent(0, sx0, xr0)
    sent(2, rs, rr)
    sent(3, sx1, xr1)
    sent(4, sg, gr1)
    sent(5, s_send, s_recv)


def body(inputs, entering, weight_in, weight_out, gate_probs, expert_ids):
    anyspace = pl.BlockSpec(memory_space=pl.ANY)
    vmem = pl.BlockSpec(memory_space=pltpu.VMEM)
    wide = pltpu.VMEM((ROWS, WIDE), BF16)
    weight = pltpu.VMEM((FF, D), BF16)
    grad = jax.ShapeDtypeStruct((FF, D), BF16)
    chunk = pltpu.VMEM((2, 2, HALF, D), BF16)
    hid = pltpu.VMEM((2, 2, FF, HALF), BF16)
    g_in, g_out, p_out = pl.pallas_call(
        kernel,
        out_shape=(grad, grad, jax.ShapeDtypeStruct((2, TOK, 2), BF16)),
        in_specs=[anyspace] * 4 + [vmem] * 2,
        out_specs=(anyspace, anyspace, vmem),
        scratch_shapes=[
            pltpu.VMEM((2, TOK, D), BF16), pltpu.VMEM((TOK, D), BF16), weight, weight,
            wide, wide, wide, wide,
            wide, wide, wide, wide, wide,
            chunk, chunk, hid, hid,
            pltpu.VMEM((2, FF, HALF), F32), pltpu.VMEM((HALF, FF), BF16),
            pltpu.VMEM((64, D), BF16),
            pltpu.VMEM((FF, D), F32), pltpu.VMEM((FF, D), F32), weight, weight,
            pltpu.VMEM((TOK, D), BF16), pltpu.VMEM((TOK, D), BF16),
            pltpu.VMEM((ROWS, 128), BF16), pltpu.VMEM((ROWS, 128), BF16),
            pltpu.VMEM((3, ROWS, TOK), BF16), pltpu.VMEM((3, ROWS, TOK), BF16),
            pltpu.VMEM((3, TOK, ROWS), BF16), pltpu.VMEM((2, TOK, 128), F32),
            pltpu.SemaphoreType.DMA((6, PEERS)), pltpu.SemaphoreType.DMA((6, PEERS)),
            pltpu.SemaphoreType.DMA, pltpu.SemaphoreType.DMA,
            pltpu.SemaphoreType.DMA((4,)), pltpu.SemaphoreType.DMA((2, 8)),
        ],
        compiler_params=pltpu.CompilerParams(
            collective_id=0, has_side_effects=True, vmem_limit_bytes=64 * 1024 * 1024 - 65536
        ),
        name="relay",
    )(inputs[0], entering[0], weight_in[0, 0], weight_out[0, 0], gate_probs[0], expert_ids[0])
    return (g_in[None, None], g_out[None, None], p_out[None])


def solution(mesh):
    return jax.shard_map(
        body,
        mesh=mesh,
        in_specs=(
            P("segment", None, "expert", None),
            P("segment", "expert", None),
            P("segment", "expert", None, None),
            P("segment", "expert", None, None),
            P("segment", None, "expert", None),
            P("segment", None, "expert", None),
        ),
        out_specs=(
            P("segment", "expert", None, None),
            P("segment", "expert", None, None),
            P("segment", None, "expert", None),
        ),
        check_vma=False,
    )
```

time: 278 us -> 131 us (0.47)
  Pallas kernels: 0 us -> 119 us
  waiting for transfers between devices: 110 us -> 0 us
  matrix products: 58.6 us -> 0 us
  starting transfers between devices: 51.8 us -> 0 us
  local copies, waits for them, and re-layouts: 41.3 us -> 9.89 us
  blocking collectives: 10.7 us -> 0 us
  other arithmetic: 2.96 us -> 0 us
    pallas_call x0 -> x1, Pallas kernels: none -> 119 us  [body(): pl.pallas_call(kernel, out_shape=(grad, grad, jax.ShapeDtypeStruct((2, TO...]
    all_to_all x8 -> x0, waiting for transfers between devices: 95.7 us -> none  [the longest x2 36.8 us: body(): lax.all_to_all(slots_g, 'expert', split_axis=0, concat_axis=0, tiled=True)]
    dot_general x14 -> x0, matrix products: 58.6 us -> none  [the longest x2 13 us: expert_pass(): lax.dot_general(hidden, grad_y, contract_rows, preferred_element_type=jnp...]
    all_to_all x8 -> x0, starting transfers between devices: 50.3 us -> none  [the longest x2 15.1 us: body(): lax.all_to_all(slots_x, 'expert', split_axis=0, concat_axis=0, tiled=True)]
    reshape x10 -> x0, local copies, waits for them, and re-layouts: 36.1 us -> none  [the longest x2 7.29 us: body(): arrived_x.reshape(slot_count, features)]
    ppermute x1 -> x0, waiting for transfers between devices: 14 us -> none  [passed_along(): return lax.ppermute(block, axis, route)]
    all_to_all x1 -> x0, blocking collectives: 10.7 us -> none  [body(): lax.all_to_all(slots_p, 'expert', split_axis=0, concat_axis=0, tiled=True)]
    unnamed x18 -> x7, local copies, waits for them, and re-layouts: 0.26 us -> 9.89 us
  transfers between devices with their start and end apart: 9 -> 0, of which waited for: 9 -> 0; matrix products, arithmetic and copies ran while one was open for 19% -> 0% of each run, Pallas kernels for 0% -> 0%
where the time goes in v1:
time: 131 us; the launch traced here: 129 us
  Pallas kernels  119 us (91%)
  local copies, waits for them, and re-layouts  9.89 us (8%)
    pallas_call x1, Pallas kernels, body(): pl.pallas_call(kernel, out_shape=(grad, grad, jax.ShapeDtypeStruct((2, TO...  119 us
    unnamed x7, local copies, waits for them, and re-layouts  9.89 us

profile of v1, /device:TPU:1, one launch (start us, length us, event | category | flops | bytes accessed | tf_op | source)
XLA Modules:
  0.0 129.2 jit_solution(14380198341290572657)
XLA Ops:
  0.6 1.4 %copy.9 = bf16[1,2,128,2]{3,2,1,0:T(8,128)(2,1)} copy(bf16[1,2,128,2]{2,3,1,0:T(2,128)(2,1)} %param.10) | data formatting | bytes 2048 | tf_op args[4]
  2.1 1.5 %copy.10 = s32[1,2,128,2]{3,2,1,0:T(8,128)} copy(s32[1,2,128,2]{2,3,1,0:T(2,128)} %param.11) | data formatting | bytes 4096 | tf_op args[5]
  3.5 118.7 %relay.1 = (bf16[704,2048]{1,0:T(8,128)(2,1)}, bf16[704,2048]{1,0:T(8,128)(2,1)}, bf16[2,128,2]{2,1,0:T(8,128)(2,1)}) custom-call(bf16[2,128,2048]{2,1,0:T(8,128)(2,1)} %bitcast.13, bf16[128,2048]{1,0:T(8,128)(2,1)} %bitcast.14, bf16[704,2048]{1,0:T(8,128)(2,1)} %bitcast.9, bf16[704,2048]{1,0:T(8,128)(2,1)} %bitcast.10, bf16[2,128,2]{2,1,0:T(8,128)(2,1)} %bitcast.16, ...), custom_call_target="tpu_custom_call" | custom-call | tf_op jit(solution)/shard_map/relay/pallas_call | solution.py:370
  122.2 1.5 %copy.11 = bf16[1,2,128,2]{2,3,1,0:T(2,128)(2,1)} copy(bf16[1,2,128,2]{3,2,1,0:T(8,128)(2,1)} %bitcast.17) | data formatting | bytes 2048
  123.7 0.0 copy-start
  123.7 3.9 %copy.14 = bf16[1,1,704,2048]{3,2,1,0:T(8,128)(2,1)} copy(bf16[1,1,704,2048]{3,2,1,0:T(8,128)(2,1)} %bitcast.12) | data formatting | bytes 5767168
  127.6 0.0 copy-done
  127.6 1.6 %copy.15 = bf16[1,1,704,2048]{3,2,1,0:T(8,128)(2,1)} copy(bf16[1,1,704,2048]{3,2,1,0:T(8,128)(2,1)S(1)} %bitcast.11) | data formatting | bytes 5767168
Async XLA Ops:
  123.7 3.9 %copy-start = (bf16[704,2048]{1,0:T(8,128)(2,1)S(1)}, bf16[704,2048]{1,0:T(8,128)(2,1)}, u32[]{:S(2)}) copy-start(bf16[704,2048]{1,0:T(8,128)(2,1)} %get-tuple-element.7) | copy-start | bytes 8650756

commit v2 on v1

--- a/solution.py
+++ b/solution.py
@@ -38,15 +38,15 @@
 
 def kernel(
     inputs_hbm, entering_hbm, win_hbm, wout_hbm, probs_ref, ids_ref,
-    gin_hbm, gout_hbm, pg_ref,
+    gin_ref, gout_ref, pg_ref,
     xin, g0, win, wout,
     sx0, sg, sx1, rs,
     xr0, gr0, xr1, rr, gr1,
     xc, gc, ht, gp, slope, gpr, rb,
-    acco, acci, outo, outi,
+    acco, acci,
     lv_send, lv_recv, s_send, s_recv,
     da, dap, ca, cols,
-    send_sem, recv_sem, z_send, z_recv, local_sem, out_sem,
+    send_sem, recv_sem, z_send, z_recv, local_sem,
 ):
     me = lax.axis_index("expert")
     seg = lax.axis_index("segment")
@@ -116,18 +116,23 @@
     pl.semaphore_signal(barrier, inc=1, device_id=(above, me), device_id_type=MESH)
 
     def places(tick):
-        ids = ids_ref[tick]
+        row = iota((8, 128), 0)
+        ids = ids_ref[tick].astype(F32)
+        odds = probs_ref[tick].astype(F32)
+        table = jnp.where(row == 0, ids[0:1], jnp.where(row == 1, ids[1:2], 0.0))
+        table = jnp.where(row == 2, odds[0:1], jnp.where(row == 3, odds[1:2], table))
+        turn = onehot(iota((TOK, 128), 0) == iota((TOK, 128), 1)).astype(BF16)
+        columns = dot_nt(turn, table.astype(BF16))
         k = iota((TOK, 128), 1)
         dx = (k >> 1) & 3
         dy = ((k >> 3) + dx) & 3
         owner = ((py + dy) & 3) * 8 + ((px + dx) & 3) * 2 + ((core + (k & 1)) & 1)
-        owner = jnp.where(k < PEERS, owner, -1)
-        named = [ids[:, j : j + 1] == owner for j in range(2)]
+        owner = jnp.where(k < PEERS, owner, -1).astype(F32)
+        named = [columns[:, j : j + 1] == owner for j in range(2)]
         either = onehot(named[0] | named[1]).astype(BF16)
         earlier = onehot(iota((TOK, TOK), 1) < iota((TOK, TOK), 0)).astype(BF16)
         count = dot(earlier, either)
         first = (k * 8).astype(F32)
-        probs = probs_ref[tick].astype(F32)
         packed = jnp.zeros((TOK, 128), F32)
         for j in range(2):
             rank = jnp.sum(jnp.where(named[j], count, 0.0), axis=1, keepdims=True)
@@ -136,7 +141,7 @@
             high = jnp.where(rank < 8.0, -100.0, base + rank - 8.0)
             packed = jnp.where(k == j, low, packed)
             packed = jnp.where(k == 2 + j, high, packed)
-            packed = jnp.where(k == 4 + j, probs[:, j : j + 1], packed)
+            packed = jnp.where(k == 4 + j, columns[:, 2 + j : 3 + j], packed)
         cols[tick] = packed
         eye = onehot(iota((8, 128), 0) == iota((8, 128), 1)).astype(BF16)
         turned = dot_nt(eye, packed.astype(BF16))
@@ -322,10 +327,8 @@
 
     def last_sums(n, carry):
         c = pl.ds(pl.multiple_of(n * 256, 256), 256)
-        outo[:, c] = (acco[:, c] + dot(ht[1, 1], gc[1, 1, :, c])).astype(BF16)
-        outi[:, c] = (acci[:, c] + dot(gp[1, 1], xc[1, 1, :, c])).astype(BF16)
-        pltpu.make_async_copy(outo.at[:, c], gout_hbm.at[:, c], out_sem.at[0, n]).start()
-        pltpu.make_async_copy(outi.at[:, c], gin_hbm.at[:, c], out_sem.at[1, n]).start()
+        gout_ref[:, c] = (acco[:, c] + dot(ht[1, 1], gc[1, 1, :, c])).astype(BF16)
+        gin_ref[:, c] = (acci[:, c] + dot(gp[1, 1], xc[1, 1, :, c])).astype(BF16)
         return carry
 
     lax.fori_loop(0, 8, last_sums, 0)
@@ -333,24 +336,19 @@
     arrive(5, s_send, s_recv, 0, PEERS)
     lane = iota((TOK, 128), 1)
     score = s_recv[...]
+    found = jnp.zeros((TOK, 128), F32)
     for tick in range(2):
-        found = []
         for j in range(2):
             va = dot(onehot(pick(tick, j, 0)).astype(BF16), score)
             vb = dot(onehot(pick(tick, j, 1)).astype(BF16), score)
             both = jnp.where(lane == tick, va, 0.0) + jnp.where(lane == 2 + tick, vb, 0.0)
-            value = jnp.sum(both, axis=1, keepdims=True)
-            found.append(value / cols[tick, :, 4 + j : 5 + j])
-        pair = jnp.where(iota((TOK, 2), 1) == 0, found[0], found[1])
-        pg_ref[tick] = pair.astype(BF16)
-
-    def out_done(n, carry):
-        c = pl.ds(pl.multiple_of(n * 256, 256), 256)
-        pltpu.make_async_copy(outo.at[:, c], gout_hbm.at[:, c], out_sem.at[0, n]).wait()
-        pltpu.make_async_copy(outi.at[:, c], gin_hbm.at[:, c], out_sem.at[1, n]).wait()
-        return carry
-
-    lax.fori_loop(0, 8, out_done, 0)
+            value = jnp.sum(both, axis=1, keepdims=True) / cols[tick, :, 4 + j : 5 + j]
+            found = jnp.where(lane == 2 * tick + j, value, found)
+    eye = onehot(iota((8, 128), 0) == iota((8, 128), 1)).astype(BF16)
+    turned = dot_nt(eye, found.astype(BF16)).astype(BF16)
+    for tick in range(2):
+        pg_ref[tick] = turned[2 * tick : 2 * tick + 2]
+
     relay.wait_send()
     sent(0, sx0, xr0)
     sent(2, rs, rr)
@@ -364,14 +362,14 @@
     vmem = pl.BlockSpec(memory_space=pltpu.VMEM)
     wide = pltpu.VMEM((ROWS, WIDE), BF16)
     weight = pltpu.VMEM((FF, D), BF16)
-    grad = jax.ShapeDtypeStruct((FF, D), BF16)
+    grad = pltpu.VMEM((FF, D), BF16)
     chunk = pltpu.VMEM((2, 2, HALF, D), BF16)
     hid = pltpu.VMEM((2, 2, FF, HALF), BF16)
     g_in, g_out, p_out = pl.pallas_call(
         kernel,
-        out_shape=(grad, grad, jax.ShapeDtypeStruct((2, TOK, 2), BF16)),
+        out_shape=(grad, grad, pltpu.VMEM((2, 2, TOK), BF16)),
         in_specs=[anyspace] * 4 + [vmem] * 2,
-        out_specs=(anyspace, anyspace, vmem),
+        out_specs=(vmem, vmem, vmem),
         scratch_shapes=[
             pltpu.VMEM((2, TOK, D), BF16), pltpu.VMEM((TOK, D), BF16), weight, weight,
             wide, wide, wide, wide,
@@ -379,21 +377,22 @@
             chunk, chunk, hid, hid,
             pltpu.VMEM((2, FF, HALF), F32), pltpu.VMEM((HALF, FF), BF16),
             pltpu.VMEM((64, D), BF16),
-            pltpu.VMEM((FF, D), F32), pltpu.VMEM((FF, D), F32), weight, weight,
+            pltpu.VMEM((FF, D), F32), pltpu.VMEM((FF, D), F32),
             pltpu.VMEM((TOK, D), BF16), pltpu.VMEM((TOK, D), BF16),
             pltpu.VMEM((ROWS, 128), BF16), pltpu.VMEM((ROWS, 128), BF16),
             pltpu.VMEM((3, ROWS, TOK), BF16), pltpu.VMEM((3, ROWS, TOK), BF16),
             pltpu.VMEM((3, TOK, ROWS), BF16), pltpu.VMEM((2, TOK, 128), F32),
             pltpu.SemaphoreType.DMA((6, PEERS)), pltpu.SemaphoreType.DMA((6, PEERS)),
             pltpu.SemaphoreType.DMA, pltpu.SemaphoreType.DMA,
-            pltpu.SemaphoreType.DMA((4,)), pltpu.SemaphoreType.DMA((2, 8)),
+            pltpu.SemaphoreType.DMA((4,)),
         ],
         compiler_params=pltpu.CompilerParams(
-            collective_id=0, has_side_effects=True, vmem_limit_bytes=64 * 1024 * 1024 - 65536
+            collective_id=0, has_side_effects=True, vmem_limit_bytes=48 * 1024 * 1024
         ),
         name="relay",
-    )(inputs[0], entering[0], weight_in[0, 0], weight_out[0, 0], gate_probs[0], expert_ids[0])
-    return (g_in[None, None], g_out[None, None], p_out[None])
+    )(inputs[0], entering[0], weight_in[0, 0], weight_out[0, 0],
+      jnp.swapaxes(gate_probs[0], 1, 2), jnp.swapaxes(expert_ids[0], 1, 2))
+    return (g_in[None, None], g_out[None, None], jnp.swapaxes(p_out, 1, 2)[None])
 
 
 def solution(mesh):

time: 131 us -> 125 us (0.954)
  local copies, waits for them, and re-layouts: 9.89 us -> 5.07 us
    unnamed x7, local copies, waits for them, and re-layouts: 9.89 us -> 5.07 us
where the time goes in v2:
time: 125 us; the launch traced here: 124 us
  Pallas kernels  118 us (94%)
  local copies, waits for them, and re-layouts  5.07 us (4%)
    pallas_call x1, Pallas kernels, body(): pl.pallas_call(kernel, out_shape=(grad, grad, pltpu.VMEM((2, 2, TOK), BF1...  118 us
    unnamed x7, local copies, waits for them, and re-layouts  5.07 us

profile of v2, /device:TPU:1, one launch (start us, length us, event | category | flops | bytes accessed | tf_op | source)
XLA Modules:
  0.0 123.7 jit_solution(15603872698881330978)
XLA Ops:
  0.6 0.0 copy-start
  0.6 0.7 copy-done
  1.3 0.0 copy-start.1
  1.3 0.7 copy-done.1
  2.0 118.0 %relay.1 = (bf16[704,2048]{1,0:T(8,128)(2,1)S(1)}, bf16[704,2048]{1,0:T(8,128)(2,1)S(1)}, bf16[2,2,128]{2,1,0:T(2,128)(2,1)S(1)}) custom-call(bf16[2,128,2048]{2,1,0:T(8,128)(2,1)} %bitcast.22, bf16[128,2048]{1,0:T(8,128)(2,1)} %bitcast.23, bf16[704,2048]{1,0:T(8,128)(2,1)} %bitcast.20, bf16[704,2048]{1,0:T(8,128)(2,1)} %bitcast.21, ...), custom_call_target="tpu_custom_call" | custom-call | tf_op jit(solution)/shard_map/relay/pallas_call | solution.py:368
  120.0 1.6 %copy.12 = bf16[1,1,704,2048]{3,2,1,0:T(8,128)(2,1)} copy(bf16[1,1,704,2048]{3,2,1,0:T(8,128)(2,1)S(1)} %bitcast.16) | data formatting | bytes 5767168
  121.6 1.6 %copy.13 = bf16[1,1,704,2048]{3,2,1,0:T(8,128)(2,1)} copy(bf16[1,1,704,2048]{3,2,1,0:T(8,128)(2,1)S(1)} %bitcast.15) | data formatting | bytes 5767168
  123.2 0.6 copy.14
Async XLA Ops:
  0.6 0.7 copy-start
  1.3 0.7 copy-start.1
